TPU v7x, 32 devices: a whole 2x2x4 slice. The times are simulated.
32 devices in a mesh: groups: 2 (over y), chan: 4 (over z), blk: 2 (over x), dir: 2 (over core).
Axes of the slice: x: 2, y: 2, z: 4, core: 2. Of those that a mesh axis runs over, the one named last changes fastest.
Arguments:
- visibilities: float32 [16, 8, 2, 512], P('groups', 'chan', 'blk'), parts along dimension 0, may hold values from -6 to 6
- antenna_pairs: int32 [2, 2, 512], P(None, 'blk'), may hold values from 0 to 511, as said below
- valid_mask: int32 [2, 1024], P('blk', 'groups'), parts along dimension 1, may hold values 0 or 1
- station_positions: float32 [2, 512], replicated, may hold values from -20 to 20
- source_offsets: float32 [2, 256], replicated, may hold values from -0.3 to 0.3
- brightness: float32 [4, 256], replicated, may hold values from -0.375 to 0.375
- source_cluster: int32 [256], replicated, may hold values from 0 to 15
- jones_gains: float32 [16, 16, 512], P('dir', 'groups'), parts along dimension 1, may hold values from -3 to 3
Outputs:
- residuals: float32 [16, 8, 2, 512], P('groups', None, 'blk', 'chan'), parts along dimension 0
- solved_gains: float32 [16, 16, 512], P('dir', 'groups'), parts along dimension 1
There are 2 independent parts, one for each index of `groups`. A program takes and returns all parts, laid end to end along the dimension named above; an argument that names none is the same for every part. Nothing has to cross between parts.
Inputs may be any that keep to these rules, and one draw needn't show every extreme that they name: `antenna_pairs`: the two stations of a baseline differ.
All inputs are finite; a program needn't handle non-finite values. No bound on the sum of `valid_mask` on one device may be relied on, other than what follows from the above.
Results may differ from a plain program's by a relative error of at most 0.0003.
Values sent between devices are 32-bit elements; how exact they have to be, the bound alone decides.
No kernel may reach another device: no remote copies, remote signals or barrier semaphores. Data moves between devices by JAX's collectives and lax.ppermute only.
A program may use at most 64 MiB of HBM per device.

v0:
```python
import math
import jax
import jax.numpy as jnp
from jax import lax
from jax.sharding import PartitionSpec as P

ITERS = 2
TWO_PI = 2.0 * math.pi
STEP_SIZE = 0.3
EPSILON = 1e-06
HIGHEST = lax.Precision.HIGHEST


def jones_product(former, latter):
    real_list = []
    imag_list = []
    for row_number in (0, 1):
        for column in (0, 1):
            real_list.append(
                former[2 * row_number] * latter[column]
                - former[4 + 2 * row_number] * latter[4 + column]
                + former[2 * row_number + 1] * latter[2 + column]
                - former[5 + 2 * row_number] * latter[6 + column]
            )
            imag_list.append(
                former[2 * row_number] * latter[4 + column]
                + former[4 + 2 * row_number] * latter[column]
                + former[2 * row_number + 1] * latter[6 + column]
                + former[5 + 2 * row_number] * latter[2 + column]
            )
    return jnp.stack(real_list + imag_list)


def adjoint(matrix):
    return jnp.stack(
        [matrix[0], matrix[2], matrix[1], matrix[3], -matrix[4], -matrix[6], -matrix[5], -matrix[7]]
    )


def source_table(brightness, source_cluster, direction_ids):
    member = (source_cluster[None, :] == direction_ids[:, None]).astype(jnp.float32)
    return (brightness[:, None, :] * member[None, :, :]).reshape(
        4 * direction_ids.shape[0], brightness.shape[1]
    )


def coherency(bright_table, geometry, scales):
    phase_grid = (TWO_PI * scales)[None, :, None] * geometry[:, None, :]
    phases_flat = phase_grid.reshape(geometry.shape[0], -1)
    real_block = jnp.dot(bright_table, jnp.cos(phases_flat), precision=HIGHEST)
    imag_block = -jnp.dot(bright_table, jnp.sin(phases_flat), precision=HIGHEST)
    dir_count = bright_table.shape[0] // 4
    return jnp.concatenate([real_block, imag_block], axis=0).reshape(
        8, dir_count, scales.shape[0], geometry.shape[1]
    )


def per_device(
    visibilities,
    antenna_pairs,
    valid_mask,
    station_positions,
    source_offsets,
    brightness,
    source_cluster,
    jones_gains,
):
    relay_count = lax.axis_size("chan")
    base_count = antenna_pairs.shape[2] // relay_count
    station_count = station_positions.shape[1]
    offset = lax.axis_index("chan") * base_count
    own_pairs = lax.dynamic_slice_in_dim(antenna_pairs[:, 0], offset, base_count, 1)
    first_station = own_pairs[0]
    second_station = own_pairs[1]
    weight_row = lax.dynamic_slice_in_dim(valid_mask[0], offset, base_count, 0).astype(jnp.float32)
    regrouped = lax.all_to_all(visibilities, "chan", split_axis=3, concat_axis=1, tiled=True)[
        :, :, 0, :
    ]
    total_channels = regrouped.shape[1]
    own_directions = jones_gains.shape[0]
    channel_ids = jnp.arange(total_channels)
    gains_now = jones_gains
    direction_ids = lax.axis_index("dir") * own_directions + jnp.arange(own_directions)
    local_channels = regrouped.shape[1]
    scales = 1.0 + 0.5 * channel_ids.astype(jnp.float32) / total_channels
    u_coord = station_positions[0][first_station] - station_positions[0][second_station]
    v_coord = station_positions[1][first_station] - station_positions[1][second_station]
    geometry = (
        source_offsets[0][:, None] * u_coord[None, :]
        + source_offsets[1][:, None] * v_coord[None, :]
    )
    bright_table = source_table(brightness, source_cluster, direction_ids)
    group_size = math.gcd(local_channels, max(1, 2048 // base_count))
    group_count = local_channels // group_size
    scale_groups = scales.reshape(group_count, group_size)
    onehot_first = (first_station[:, None] == jnp.arange(station_count)[None, :]).astype(
        jnp.float32
    )
    onehot_second = (second_station[:, None] == jnp.arange(station_count)[None, :]).astype(
        jnp.float32
    )

    def station_gains(gains_current):
        gain_first = jnp.take(gains_current, first_station, axis=2).transpose(1, 0, 2)[
            :, :, None, :
        ]
        gain_second = jnp.take(gains_current, second_station, axis=2).transpose(1, 0, 2)[
            :, :, None, :
        ]
        return (gain_first, gain_second)

    def residual_of(gains_current):
        gain_first, gain_second = station_gains(gains_current)

        def residual_one_group(scale_group):
            coherent = coherency(bright_table, geometry, scale_group)
            return jnp.sum(
                jones_product(jones_product(gain_first, coherent), adjoint(gain_second)), axis=1
            )

        partial_model = jnp.moveaxis(lax.map(residual_one_group, scale_groups), 0, 1).reshape(
            8, local_channels, base_count
        )
        model_vis = lax.psum(partial_model, "dir")
        return weight_row * (regrouped - model_vis)

    for iteration in range(ITERS):
        residual_now = residual_of(gains_now)
        updated_gain_first, updated_gain_second = station_gains(gains_now)
        resid_groups = jnp.moveaxis(
            residual_now.reshape(8, group_count, group_size, base_count), 1, 0
        )
        dir_count = gains_now.shape[0]

        def updated_one_group(running, inputs):
            scale_group, resid_group = inputs
            coherent = coherency(bright_table, geometry, scale_group)
            toward_second = jones_product(updated_gain_second, adjoint(coherent))
            toward_first = jones_product(updated_gain_first, coherent)
            grad_first = jnp.sum(jones_product(resid_group[:, None], toward_second), axis=2)
            grad_second = jnp.sum(
                jones_product(adjoint(resid_group)[:, None], toward_first), axis=2
            )
            curv_first = jnp.sum(toward_second * toward_second, axis=(0, 2))
            curv_second = jnp.sum(toward_first * toward_first, axis=(0, 2))
            return (
                (
                    running[0] + grad_first,
                    running[1] + grad_second,
                    running[2] + curv_first,
                    running[3] + curv_second,
                ),
                None,
            )

        zero_sums = (
            jnp.zeros((8, dir_count, base_count), jnp.float32),
            jnp.zeros((8, dir_count, base_count), jnp.float32),
            jnp.zeros((dir_count, base_count), jnp.float32),
            jnp.zeros((dir_count, base_count), jnp.float32),
        )
        totals, ignored = lax.scan(updated_one_group, zero_sums, (scale_groups, resid_groups))
        grad_station = jnp.einsum(
            "cdb,bs->dcs", totals[0], onehot_first, precision=HIGHEST
        ) + jnp.einsum("cdb,bs->dcs", totals[1], onehot_second, precision=HIGHEST)
        curv_station = jnp.dot(weight_row * totals[2], onehot_first, precision=HIGHEST) + jnp.dot(
            weight_row * totals[3], onehot_second, precision=HIGHEST
        )
        grad_station, curv_station = lax.psum((grad_station, curv_station), ("chan", "blk"))
        gains_now = gains_now + STEP_SIZE * grad_station / (curv_station[:, None, :] + EPSILON)
    residual_now = residual_of(gains_now)
    return (residual_now[:, :, None, :], gains_now)


def solution(mesh):
    in_specs = (
        P("groups", "chan", "blk", None),
        P(None, "blk", None),
        P("blk", "groups"),
        P(),
        P(),
        P(),
        P(),
        P("dir", "groups", None),
    )
    out_specs = (P("groups", None, "blk", "chan"), P("dir", "groups", None))
    return jax.shard_map(
        per_device, mesh=mesh, in_specs=in_specs, out_specs=out_specs, check_vma=False
    )
```

profile of v0, /device:TPU:0, one launch (start us, length us, event | category | flops | bytes accessed | tf_op | source)
XLA Modules:
  0.0 311.1 jit_solution(10712981869981205140)
XLA Ops:
  7.2 1.0 copy.374
  8.2 1.4 reshape.6361
  9.6 6.3 %all-to-all-start = ((f32[4,1,2048]{2,1,0:T(1,128)}), f32[4,1,2048]{2,1,0:T(1,128)S(1)}, u32[]{:S(2)}, u32[]{:S(2)}) async-start(f32[4,1,2048]{2,1,0:T(1,128)} %reshape.6361), calls=%async_computation | async-start | bytes 65536 | tf_op jit(solution)/shard_map/all_to_all | solution.py:76
  17.3 0.8 fusion.56
  18.0 1.3 gather_fusion.3
  19.3 1.3 gather_fusion.1
  20.6 1.3 gather_fusion
  21.9 1.4 gather_fusion.2
  24.4 3.7 %multiply_cosine_fusion = (f32[256,8,128]{2,1,0:T(8,128)S(1)}, f32[256,8,128]{2,1,0:T(8,128)S(1)}) fusion(f32[256,128]{1,0:T(8,128)S(1)} %multiply_add_fusion, f32[8]{0:T(128)S(1)} %add_multiply_fusion), kind=kLoop, calls=%fused_computation.11 | loop fusion | flops 262144 | bytes 2228256 | tf_op jit(solution)/shard_map/while/body/eval_jaxpr/cos | solution.py:50
  28.1 0.8 fusion.4
  28.9 0.8 convolution_negate_fusion
  30.5 0.8 gather_fusion.5
  31.3 1.6 gather_fusion.4
  33.0 2.0 fusion.55
  35.0 1.2 copy.387
  36.2 1.2 copy.390
  39.1 2.0 fusion.54
  41.1 1.2 copy.391
  42.3 1.2 copy.394
  46.2 37.6 %psum.51 = f32[8,512]{1,0:T(8,128)S(1)} all-reduce(f32[8,512]{1,0:T(8,128)S(1)} %convolution_add_fusion.3), channel_id=1, replica_groups=mesh['groups'=2,'chan'=4,'blk'=2,'dir'=2] {'chan','blk'}, use_global_device_ids=true, to_apply=%region_7.9 | all-reduce | flops 4096 | bytes 32768 | tf_op jit(solution)/shard_map/psum | solution.py:169
  83.7 3.6 %psum.49 = f32[8,8,128]{2,1,0:T(8,128)S(1)} all-reduce(f32[8,8,128]{2,1,0:T(8,128)S(1)} %reduce_sum.110), channel_id=1, replica_groups=mesh['groups'=2,'chan'=4,'blk'=2,'dir'=2] {'dir'}, use_global_device_ids=true, to_apply=%region_1.3 | all-reduce | flops 8192 | bytes 65536 | tf_op jit(solution)/shard_map/psum | solution.py:124
  88.6 0.8 reshape.6362
  91.0 1.0 fusion.1
  92.0 67.1 %all-reduce.3.cloned.1.call-done = f32[8,8,512]{2,0,1:T(8,128)} async-done(((f32[8,8,512]{2,0,1:T(8,128)}), f32[8,8,512]{2,0,1:T(8,128)}) %all-reduce.3.cloned.1.call-update) | async-done | bytes 131088 | tf_op jit(solution)/shard_map/psum | solution.py:169
  159.1 1.0 copy_add_fusion
  160.1 0.8 copy.397
  160.9 0.8 gather_fusion.7
  161.7 0.8 gather_fusion.6
  162.9 2.1 fusion.53
  165.0 1.2 copy.407
  166.3 1.2 copy.410
  168.1 1.2 copy.408
  172.3 2.2 fusion.52
  174.4 1.2 copy.411
  175.7 1.2 copy.414
  176.9 1.2 copy.413
  181.1 35.4 %psum.54 = f32[8,512]{1,0:T(8,128)S(1)} all-reduce(f32[8,512]{1,0:T(8,128)S(1)} %convolution_add_fusion.2), channel_id=1, replica_groups=mesh['groups'=2,'chan'=4,'blk'=2,'dir'=2] {'chan','blk'}, use_global_device_ids=true, to_apply=%region_15.17 | all-reduce | flops 4096 | bytes 32768 | tf_op jit(solution)/shard_map/psum | solution.py:169
  216.8 3.7 %psum.52 = f32[8,8,128]{2,1,0:T(8,128)S(1)} all-reduce(f32[8,8,128]{2,1,0:T(8,128)S(1)} %reduce_sum.115), channel_id=1, replica_groups=mesh['groups'=2,'chan'=4,'blk'=2,'dir'=2] {'dir'}, use_global_device_ids=true, to_apply=%region_9.11 | all-reduce | flops 8192 | bytes 65536 | tf_op jit(solution)/shard_map/psum | solution.py:124
  221.3 1.0 fusion
  222.3 67.1 %all-reduce.5.cloned.1.call-done = f32[8,8,512]{2,0,1:T(8,128)} async-done(((f32[8,8,512]{2,0,1:T(8,128)}), f32[8,8,512]{2,0,1:T(8,128)}) %all-reduce.5.cloned.1.call-update) | async-done | bytes 131088 | tf_op jit(solution)/shard_map/psum | solution.py:169
  289.4 0.9 divide_add_fusion
  291.1 0.8 copy.416
  291.9 0.9 gather_fusion.9
  292.8 0.9 gather_fusion.8
  294.1 2.0 fusion.51
  296.1 1.2 copy.423
  297.3 1.2 copy.426
  300.2 3.4 %psum.55 = f32[8,8,128]{2,1,0:T(8,128)S(1)} all-reduce(f32[8,8,128]{2,1,0:T(8,128)S(1)} %reduce_sum.120), channel_id=1, replica_groups=mesh['groups'=2,'chan'=4,'blk'=2,'dir'=2] {'dir'}, use_global_device_ids=true, to_apply=%region_17.19 | all-reduce | flops 8192 | bytes 65536 | tf_op jit(solution)/shard_map/psum | solution.py:124
  (244 shorter events, 21.1 us)
Async XLA Ops:
  7.2 16.9 %copy-start.32 = (f32[2,256]{1,0:T(2,128)S(1)}, f32[2,256]{1,0:T(2,128)}, u32[]{:S(2)}) copy-start(f32[2,256]{1,0:T(2,128)} %param.14) | copy-start | bytes 6148
  7.2 17.0 %copy-start.37 = (s32[256]{0:T(256)S(1)}, s32[256]{0:T(256)}, u32[]{:S(2)}) copy-start(s32[256]{0:T(256)} %param.16) | copy-start | bytes 3076
  9.6 77.8 %all-to-all-start = ((f32[4,1,2048]{2,1,0:T(1,128)}), f32[4,1,2048]{2,1,0:T(1,128)S(1)}, u32[]{:S(2)}, u32[]{:S(2)}) async-start(f32[4,1,2048]{2,1,0:T(1,128)} %reshape.6361), calls=%async_computation | async-start | bytes 65536 | tf_op jit(solution)/shard_map/all_to_all | solution.py:76
  15.9 143.2 %all-reduce.3.cloned.1.call-start = ((), (), s32[]{:S(2)}) async-start(), calls=%async_computation.1 | async-start | bytes 262144 | tf_op jit(solution)/shard_map/psum | solution.py:169
  16.6 74.1 %copy-start.35 = (s32[128]{0:T(128)}, s32[128]{0:T(128)S(1)}, u32[]{:S(2)}) copy-start(s32[128]{0:T(128)S(1)} %get-tuple-element.223) | copy-start | bytes 1540
  16.6 145.9 %copy-start.23 = (pred[128]{0:T(512)(128)(4,1)}, pred[128]{0:T(512)(128)(4,1)S(1)}, u32[]{:S(2)}) copy-start(pred[128]{0:T(512)(128)(4,1)S(1)} %get-tuple-element.222) | copy-start | bytes 388
  17.3 73.7 %copy-start.33 = (s32[1,1,128]{2,1,0:T(1,128)}, s32[1,1,128]{2,1,0:T(1,128)S(1)}, u32[]{:S(2)}) copy-start(s32[1,1,128]{2,1,0:T(1,128)S(1)} %get-tuple-element.225) | copy-start | bytes 1540
  19.3 8.7 %copy-start.22 = (f32[4,256]{1,0:T(4,128)S(1)}, f32[4,256]{1,0:T(4,128)}, u32[]{:S(2)}) copy-start(f32[4,256]{1,0:T(4,128)} %param.15) | copy-start | bytes 12292
  24.0 65.6 %copy-start.27 = (f32[128]{0:T(128)}, f32[128]{0:T(128)S(1)}, u32[]{:S(2)}) copy-start(f32[128]{0:T(128)S(1)} %fusion.46) | copy-start | bytes 1540
  24.0 138.7 %copy-start.30 = (pred[128]{0:T(512)(128)(4,1)}, pred[128]{0:T(512)(128)(4,1)S(1)}, u32[]{:S(2)}) copy-start(pred[128]{0:T(512)(128)(4,1)S(1)} %compare_and_fusion.1) | copy-start | bytes 388
  24.1 137.6 %copy-start.25 = (s32[1024]{0:T(1024)}, s32[1024]{0:T(1024)S(1)}, u32[]{:S(2)}) copy-start(s32[1024]{0:T(1024)S(1)} %pad_clamp_fusion.3) | copy-start | bytes 12292
  24.1 136.8 %copy-start.26 = (s32[1024]{0:T(1024)}, s32[1024]{0:T(1024)S(1)}, u32[]{:S(2)}) copy-start(s32[1024]{0:T(1024)S(1)} %pad_clamp_fusion) | copy-start | bytes 12292
  24.4 5.4 %copy-start.1 = (f32[8,8,512]{2,1,0:T(8,128)S(1)}, f32[8,8,512]{2,1,0:T(8,128)}, u32[]{:S(2)}) copy-start(f32[8,8,512]{2,1,0:T(8,128)} %param.17) | copy-start | bytes 393220
  37.7 1.2 copy-start
  89.6 0.6 copy-start.3
  90.3 68.9 %copy-start.2 = (f32[8,8,512]{2,1,0:T(8,128)S(1)}, f32[8,8,512]{2,1,0:T(8,128)}, u32[]{:S(2)}) copy-start(f32[8,8,512]{2,1,0:T(8,128)} %param.17) | copy-start | bytes 393220
  91.9 197.5 %all-reduce.5.cloned.1.call-start = ((), (), s32[]{:S(2)}) async-start(), calls=%async_computation.2 | async-start | bytes 262144 | tf_op jit(solution)/shard_map/psum | solution.py:169
  167.5 4.1 %copy-start.6 = (f32[1,8,128]{2,1,0:T(8,128)}, f32[1,8,128]{2,1,0:T(8,128)S(1)}, u32[]{:S(2)}) copy-start(f32[1,8,128]{2,1,0:T(8,128)S(1)} %copy.410) | copy-start | bytes 12292
  169.3 2.5 copy-start.8
  170.2 1.9 copy-start.10
  171.0 1.1 copy-start.12
  174.4 4.9 %copy-start.11 = (f32[1,8,128]{2,1,0:T(8,128)S(1)}, f32[1,8,128]{2,1,0:T(8,128)}, u32[]{:S(2)}) copy-start(f32[1,8,128]{2,1,0:T(8,128)} %copy-done.10) | copy-start | bytes 12292
  174.4 4.9 %copy-start.13 = (f32[1,8,128]{2,1,0:T(8,128)S(1)}, f32[1,8,128]{2,1,0:T(8,128)}, u32[]{:S(2)}) copy-start(f32[1,8,128]{2,1,0:T(8,128)} %copy-done.12) | copy-start | bytes 12292
  175.7 4.4 %copy-start.14 = (f32[1,8,128]{2,1,0:T(8,128)}, f32[1,8,128]{2,1,0:T(8,128)S(1)}, u32[]{:S(2)}) copy-start(f32[1,8,128]{2,1,0:T(8,128)S(1)} %copy.411) | copy-start | bytes 12292
  176.9 3.1 %copy-start.15 = (f32[1,8,128]{2,1,0:T(8,128)}, f32[1,8,128]{2,1,0:T(8,128)S(1)}, u32[]{:S(2)}) copy-start(f32[1,8,128]{2,1,0:T(8,128)S(1)} %copy.414) | copy-start | bytes 12292
  176.9 2.5 copy-start.7
  176.9 2.5 copy-start.9
  178.2 1.9 copy-start.16
  178.4 1.7 copy-start.17
  178.6 1.1 copy-start.28
  178.6 1.1 copy-start.36
  179.1 1.8 copy-start.34
  179.3 37.3 %copy-start.20 = (f32[8,128]{1,0:T(8,128)S(1)}, f32[8,128]{1,0:T(8,128)}, u32[]{:S(2)}) copy-start(f32[8,128]{1,0:T(8,128)} %bitcast_negate_fusion.2) | copy-start | bytes 12292
  179.3 37.3 %copy-start.21 = (f32[8,128]{1,0:T(8,128)S(1)}, f32[8,128]{1,0:T(8,128)}, u32[]{:S(2)}) copy-start(f32[8,128]{1,0:T(8,128)} %bitcast_negate_fusion.3) | copy-start | bytes 12292
  179.3 37.3 %copy-start.18 = (f32[8,128]{1,0:T(8,128)S(1)}, f32[8,128]{1,0:T(8,128)}, u32[]{:S(2)}) copy-start(f32[8,128]{1,0:T(8,128)} %bitcast_negate_fusion) | copy-start | bytes 12292
  179.3 37.3 %copy-start.19 = (f32[8,128]{1,0:T(8,128)S(1)}, f32[8,128]{1,0:T(8,128)}, u32[]{:S(2)}) copy-start(f32[8,128]{1,0:T(8,128)} %bitcast_negate_fusion.1) | copy-start | bytes 12292
  179.5 41.0 %copy-start.4 = (f32[8,4,2,1,128]{4,0,2,1,3:T(8,128)S(1)}, f32[8,4,2,1,128]{4,0,2,1,3:T(8,128)}, u32[]{:S(2)}) copy-start(f32[8,4,2,1,128]{4,0,2,1,3:T(8,128)} %copy-done.3) | copy-start | bytes 98308
  221.3 72.5 %copy-start.31 = (pred[128]{0:T(512)(128)(4,1)S(1)}, pred[128]{0:T(512)(128)(4,1)}, u32[]{:S(2)}) copy-start(pred[128]{0:T(512)(128)(4,1)} %copy-done.30) | copy-start | bytes 388
  221.3 72.6 %copy-start.24 = (pred[128]{0:T(512)(128)(4,1)S(1)}, pred[128]{0:T(512)(128)(4,1)}, u32[]{:S(2)}) copy-start(pred[128]{0:T(512)(128)(4,1)} %copy-done.23) | copy-start | bytes 388
  299.2 4.5 %copy-start.5 = (f32[8,4,2,1,128]{4,0,2,1,3:T(8,128)S(1)}, f32[8,4,2,1,128]{4,0,2,1,3:T(8,128)}, u32[]{:S(2)}) copy-start(f32[8,4,2,1,128]{4,0,2,1,3:T(8,128)} %copy-done.3) | copy-start | bytes 98308
  299.2 4.5 %copy-start.29 = (f32[128]{0:T(128)S(1)}, f32[128]{0:T(128)}, u32[]{:S(2)}) copy-start(f32[128]{0:T(128)} %copy-done.27) | copy-start | bytes 1540
Sparse Core Ops, SparseCore 0:
  92.1 67.0 all-reduce.2
  222.4 66.9 all-reduce.4
where the time goes:
time: 312 us; the launch traced here: 311 us
  waiting for transfers between devices  134 us (43%)
  blocking collectives  83.7 us (27%)
  local copies, waits for them, and re-layouts  50.7 us (16%)
  other arithmetic  15.7 us (5%)
  between operations  15.3 us (5%)
  starting transfers between devices  6.36 us (2%)
  matrix products  5.15 us (2%)
    psum x2, waiting for transfers between devices, per_device(): lax.psum((grad_station, curv_station), ('chan', 'blk'))  134 us
    psum x2, blocking collectives, per_device(): lax.psum((grad_station, curv_station), ('chan', 'blk'))  73 us
    psum x3, blocking collectives, residual_of(): model_vis = lax.psum(partial_model, 'dir')  10.7 us
    slice x9, local copies, waits for them, and re-layouts, jones_product(): former[2 * row_number] * latter[column]  10.5 us
    slice x4, local copies, waits for them, and re-layouts, adjoint(): matrix[2]  6.6 us
    all_to_all x1, starting transfers between devices, per_device(): lax.all_to_all(visibilities, 'chan', split_axis=3, concat_axis=1, tiled=T...  6.32 us
  transfers between devices with their start and end apart: 3, of which 2 were waited for; matrix products, arithmetic and copies ran while one was open for 10% of the time, Pallas kernels for 0%

commit v1 on v0

--- a/solution.py
+++ b/solution.py
@@ -3,12 +3,19 @@
 import jax.numpy as jnp
 from jax import lax
 from jax.sharding import PartitionSpec as P
+from jax.lax import psum
 
 ITERS = 2
 TWO_PI = 2.0 * math.pi
 STEP_SIZE = 0.3
 EPSILON = 1e-06
 HIGHEST = lax.Precision.HIGHEST
+
+
+def connect_marks(q_in, shard_axis, peer_axis):
+    later = psum(q_in, shard_axis)
+    block_now = psum(later, peer_axis)
+    return block_now
 
 
 def jones_product(former, latter):
@@ -166,7 +173,7 @@
         curv_station = jnp.dot(weight_row * totals[2], onehot_first, precision=HIGHEST) + jnp.dot(
             weight_row * totals[3], onehot_second, precision=HIGHEST
         )
-        grad_station, curv_station = lax.psum((grad_station, curv_station), ("chan", "blk"))
+        grad_station, curv_station = connect_marks((grad_station, curv_station), "blk", "chan")
         gains_now = gains_now + STEP_SIZE * grad_station / (curv_station[:, None, :] + EPSILON)
     residual_now = residual_of(gains_now)
     return (residual_now[:, :, None, :], gains_now)

time: 312 us -> 222 us (0.71)
  waiting for transfers between devices: 134 us -> 64.2 us
  blocking collectives: 83.7 us -> 63.4 us
    psum x2 -> x4, waiting for transfers between devices: 134 us -> 64.2 us  [the longest x2 64.2 us: connect_marks(): block_now = psum(later, peer_axis)]
    psum x2 -> x4, blocking collectives: 73 us -> 53 us  [the longest x2 36.7 us: connect_marks(): block_now = psum(later, peer_axis)]
  transfers between devices with their start and end apart: 3 -> 5, of which waited for: 2 -> 2; matrix products, arithmetic and copies ran while one was open for 10% -> 14% of each run, Pallas kernels for 0% -> 0%
where the time goes in v1:
time: 222 us; the launch traced here: 221 us
  waiting for transfers between devices  64.2 us (29%)
  blocking collectives  63.4 us (29%)
  local copies, waits for them, and re-layouts  50.8 us (23%)
  other arithmetic  15.7 us (7%)
  between operations  15 us (7%)
  starting transfers between devices  6.44 us (3%)
  matrix products  5.15 us (2%)
    psum x2, waiting for transfers between devices, connect_marks(): block_now = psum(later, peer_axis)  64.2 us
    psum x2, blocking collectives, connect_marks(): block_now = psum(later, peer_axis)  36.7 us
    psum x2, blocking collectives, connect_marks(): later = psum(q_in, shard_axis)  16.3 us
    slice x9, local copies, waits for them, and re-layouts, jones_product(): former[2 * row_number] * latter[column]  10.6 us
    psum x3, blocking collectives, residual_of(): model_vis = lax.psum(partial_model, 'dir')  10.4 us
    slice x4, local copies, waits for them, and re-layouts, adjoint(): matrix[2]  6.63 us
    all_to_all x1, starting transfers between devices, per_device(): lax.all_to_all(visibilities, 'chan', split_axis=3, concat_axis=1, tiled=T...  6.32 us
    unnamed x81, local copies, waits for them, and re-layouts  5.33 us
  transfers between devices with their start and end apart: 5, of which 2 were waited for; matrix products, arithmetic and copies ran while one was open for 14% of the time, Pallas kernels for 0%

profile of v1, /device:TPU:0, one launch (start us, length us, event | category | flops | bytes accessed | tf_op | source)
XLA Modules:
  0.0 220.7 jit_solution(4735894076862289247)
XLA Ops:
  7.2 1.0 copy.374
  8.2 1.4 reshape.6361
  9.6 6.3 %all-to-all-start = ((f32[4,1,2048]{2,1,0:T(1,128)}), f32[4,1,2048]{2,1,0:T(1,128)S(1)}, u32[]{:S(2)}, u32[]{:S(2)}) async-start(f32[4,1,2048]{2,1,0:T(1,128)} %reshape.6361), calls=%async_computation | async-start | bytes 65536 | tf_op jit(solution)/shard_map/all_to_all | solution.py:83
  17.3 0.8 fusion.56
  18.0 1.3 gather_fusion.3
  19.3 1.3 gather_fusion.1
  20.6 1.3 gather_fusion
  21.9 1.4 gather_fusion.2
  24.4 3.7 %multiply_cosine_fusion = (f32[256,8,128]{2,1,0:T(8,128)S(1)}, f32[256,8,128]{2,1,0:T(8,128)S(1)}) fusion(f32[256,128]{1,0:T(8,128)S(1)} %multiply_add_fusion, f32[8]{0:T(128)S(1)} %add_multiply_fusion), kind=kLoop, calls=%fused_computation.11 | loop fusion | flops 262144 | bytes 2228256 | tf_op jit(solution)/shard_map/while/body/eval_jaxpr/cos | solution.py:57
  28.1 0.8 fusion.4
  28.9 0.8 convolution_negate_fusion
  30.5 0.8 gather_fusion.5
  31.3 1.6 gather_fusion.4
  33.0 2.0 fusion.55
  35.0 1.2 copy.387
  36.3 1.2 copy.390
  39.1 2.0 fusion.54
  41.1 1.2 copy.391
  42.3 1.2 copy.394
  45.9 3.6 %psum.77 = f32[8,8,128]{2,1,0:T(8,128)S(1)} all-reduce(f32[8,8,128]{2,1,0:T(8,128)S(1)} %reduce_sum.110), channel_id=1, replica_groups=mesh['groups'=2,'chan'=4,'blk'=2,'dir'=2] {'dir'}, use_global_device_ids=true, to_apply=%region_1.3 | all-reduce | flops 8192 | bytes 65536 | tf_op jit(solution)/shard_map/psum | solution.py:131
  50.8 0.8 reshape.6362
  53.1 1.0 fusion.1
  54.4 8.1 %psum.80 = f32[8,512]{1,0:T(8,128)S(1)} all-reduce(f32[8,512]{1,0:T(8,128)S(1)} %convolution_add_fusion.3), channel_id=1, replica_groups=mesh['groups'=2,'chan'=4,'blk'=2,'dir'=2] {'blk'}, use_global_device_ids=true, to_apply=%region_8.10 | all-reduce | flops 4096 | bytes 32768 | tf_op jit(solution)/shard_map/psum | solution.py:16
  62.6 19.2 %psum.81 = f32[8,512]{1,0:T(8,128)S(1)} all-reduce(f32[8,512]{1,0:T(8,128)S(1)} %psum.80), channel_id=1, replica_groups=mesh['groups'=2,'chan'=4,'blk'=2,'dir'=2] {'chan'}, use_global_device_ids=true, to_apply=%region_9.11 | all-reduce | flops 4096 | bytes 32768 | tf_op jit(solution)/shard_map/psum | solution.py:17
  81.9 32.1 %all-reduce.7.cloned.1.call-done = f32[8,8,512]{2,0,1:T(8,128)} async-done(((f32[8,8,512]{2,0,1:T(8,128)}), f32[8,8,512]{2,0,1:T(8,128)}) %all-reduce.7.cloned.1.call-update) | async-done | bytes 131088 | tf_op jit(solution)/shard_map/psum | solution.py:17
  113.9 1.0 copy_add_fusion
  115.7 0.8 gather_fusion.7
  116.5 0.8 gather_fusion.6
  117.7 2.2 fusion.53
  119.9 1.2 copy.407
  121.1 1.2 copy.410
  122.9 1.2 copy.408
  127.1 2.2 fusion.52
  129.3 1.2 copy.411
  130.5 1.2 copy.414
  131.8 1.2 copy.413
  136.0 3.4 %psum.82 = f32[8,8,128]{2,1,0:T(8,128)S(1)} all-reduce(f32[8,8,128]{2,1,0:T(8,128)S(1)} %reduce_sum.115), channel_id=1, replica_groups=mesh['groups'=2,'chan'=4,'blk'=2,'dir'=2] {'dir'}, use_global_device_ids=true, to_apply=%region_11.13 | all-reduce | flops 8192 | bytes 65536 | tf_op jit(solution)/shard_map/psum | solution.py:131
  140.2 1.0 fusion
  141.5 8.1 %psum.85 = f32[8,512]{1,0:T(8,128)S(1)} all-reduce(f32[8,512]{1,0:T(8,128)S(1)} %convolution_add_fusion.2), channel_id=1, replica_groups=mesh['groups'=2,'chan'=4,'blk'=2,'dir'=2] {'blk'}, use_global_device_ids=true, to_apply=%region_18.20 | all-reduce | flops 4096 | bytes 32768 | tf_op jit(solution)/shard_map/psum | solution.py:16
  149.7 17.5 %psum.86 = f32[8,512]{1,0:T(8,128)S(1)} all-reduce(f32[8,512]{1,0:T(8,128)S(1)} %psum.85), channel_id=1, replica_groups=mesh['groups'=2,'chan'=4,'blk'=2,'dir'=2] {'chan'}, use_global_device_ids=true, to_apply=%region_19.21 | all-reduce | flops 4096 | bytes 32768 | tf_op jit(solution)/shard_map/psum | solution.py:17
  167.2 32.1 %all-reduce.11.cloned.1.call-done = f32[8,8,512]{2,0,1:T(8,128)} async-done(((f32[8,8,512]{2,0,1:T(8,128)}), f32[8,8,512]{2,0,1:T(8,128)}) %all-reduce.11.cloned.1.call-update) | async-done | bytes 131088 | tf_op jit(solution)/shard_map/psum | solution.py:17
  199.3 0.9 divide_add_fusion
  201.7 0.9 gather_fusion.9
  202.6 0.9 gather_fusion.8
  204.0 2.0 fusion.51
  206.0 1.2 copy.423
  207.2 1.2 copy.426
  210.1 3.4 %psum.87 = f32[8,8,128]{2,1,0:T(8,128)S(1)} all-reduce(f32[8,8,128]{2,1,0:T(8,128)S(1)} %reduce_sum.120), channel_id=1, replica_groups=mesh['groups'=2,'chan'=4,'blk'=2,'dir'=2] {'dir'}, use_global_device_ids=true, to_apply=%region_21.23 | all-reduce | flops 8192 | bytes 65536 | tf_op jit(solution)/shard_map/psum | solution.py:131
  (252 shorter events, 22.7 us)
Async XLA Ops:
  7.2 16.9 %copy-start.32 = (f32[2,256]{1,0:T(2,128)S(1)}, f32[2,256]{1,0:T(2,128)}, u32[]{:S(2)}) copy-start(f32[2,256]{1,0:T(2,128)} %param.14) | copy-start | bytes 6148
  7.2 17.0 %copy-start.37 = (s32[256]{0:T(256)S(1)}, s32[256]{0:T(256)}, u32[]{:S(2)}) copy-start(s32[256]{0:T(256)} %param.16) | copy-start | bytes 3076
  9.6 40.0 %all-to-all-start = ((f32[4,1,2048]{2,1,0:T(1,128)}), f32[4,1,2048]{2,1,0:T(1,128)S(1)}, u32[]{:S(2)}, u32[]{:S(2)}) async-start(f32[4,1,2048]{2,1,0:T(1,128)} %reshape.6361), calls=%async_computation | async-start | bytes 65536 | tf_op jit(solution)/shard_map/all_to_all | solution.py:83
  15.9 65.9 %all-reduce.5.cloned.1.call-start = ((), (), s32[]{:S(2)}) async-start(), calls=%async_computation.1 | async-start | bytes 262144 | tf_op jit(solution)/shard_map/psum | solution.py:16
  16.6 36.2 %copy-start.35 = (s32[128]{0:T(128)}, s32[128]{0:T(128)S(1)}, u32[]{:S(2)}) copy-start(s32[128]{0:T(128)S(1)} %get-tuple-element.223) | copy-start | bytes 1540
  16.6 100.7 %copy-start.23 = (pred[128]{0:T(512)(128)(4,1)}, pred[128]{0:T(512)(128)(4,1)S(1)}, u32[]{:S(2)}) copy-start(pred[128]{0:T(512)(128)(4,1)S(1)} %get-tuple-element.222) | copy-start | bytes 388
  17.3 36.9 %copy-start.33 = (s32[1,1,128]{2,1,0:T(1,128)}, s32[1,1,128]{2,1,0:T(1,128)S(1)}, u32[]{:S(2)}) copy-start(s32[1,1,128]{2,1,0:T(1,128)S(1)} %get-tuple-element.225) | copy-start | bytes 1540
  19.3 8.7 %copy-start.22 = (f32[4,256]{1,0:T(4,128)S(1)}, f32[4,256]{1,0:T(4,128)}, u32[]{:S(2)}) copy-start(f32[4,256]{1,0:T(4,128)} %param.15) | copy-start | bytes 12292
  24.0 30.2 %copy-start.27 = (f32[128]{0:T(128)}, f32[128]{0:T(128)S(1)}, u32[]{:S(2)}) copy-start(f32[128]{0:T(128)S(1)} %fusion.46) | copy-start | bytes 1540
  24.0 93.5 %copy-start.30 = (pred[128]{0:T(512)(128)(4,1)}, pred[128]{0:T(512)(128)(4,1)S(1)}, u32[]{:S(2)}) copy-start(pred[128]{0:T(512)(128)(4,1)S(1)} %compare_and_fusion.1) | copy-start | bytes 388
  24.1 92.4 %copy-start.25 = (s32[1024]{0:T(1024)}, s32[1024]{0:T(1024)S(1)}, u32[]{:S(2)}) copy-start(s32[1024]{0:T(1024)S(1)} %pad_clamp_fusion.3) | copy-start | bytes 12292
  24.1 91.6 %copy-start.26 = (s32[1024]{0:T(1024)}, s32[1024]{0:T(1024)S(1)}, u32[]{:S(2)}) copy-start(s32[1024]{0:T(1024)S(1)} %pad_clamp_fusion) | copy-start | bytes 12292
  24.4 5.4 %copy-start.1 = (f32[8,8,512]{2,1,0:T(8,128)S(1)}, f32[8,8,512]{2,1,0:T(8,128)}, u32[]{:S(2)}) copy-start(f32[8,8,512]{2,1,0:T(8,128)} %param.17) | copy-start | bytes 393220
  37.7 1.2 copy-start
  51.8 0.6 copy-start.3
  52.5 61.5 %copy-start.2 = (f32[8,8,512]{2,1,0:T(8,128)S(1)}, f32[8,8,512]{2,1,0:T(8,128)}, u32[]{:S(2)}) copy-start(f32[8,8,512]{2,1,0:T(8,128)} %param.17) | copy-start | bytes 393220
  54.1 59.8 %all-reduce.7.cloned.1.call-start = ((), (), s32[]{:S(2)}) async-start(), calls=%async_computation.2 | async-start | bytes 262144 | tf_op jit(solution)/shard_map/psum | solution.py:17
  81.8 85.3 %all-reduce.9.cloned.1.call-start = ((), (), s32[]{:S(2)}) async-start(), calls=%async_computation.3 | async-start | bytes 262144 | tf_op jit(solution)/shard_map/psum | solution.py:16
  122.3 4.1 %copy-start.6 = (f32[1,8,128]{2,1,0:T(8,128)}, f32[1,8,128]{2,1,0:T(8,128)S(1)}, u32[]{:S(2)}) copy-start(f32[1,8,128]{2,1,0:T(8,128)S(1)} %copy.410) | copy-start | bytes 12292
  124.2 2.5 %copy-start.8 = (f32[1,8,128]{2,1,0:T(8,128)}, f32[1,8,128]{2,1,0:T(8,128)S(1)}, u32[]{:S(2)}) copy-start(f32[1,8,128]{2,1,0:T(8,128)S(1)} %copy.408) | copy-start | bytes 12292
  125.0 1.9 copy-start.10
  125.8 1.1 copy-start.12
  129.3 4.9 %copy-start.11 = (f32[1,8,128]{2,1,0:T(8,128)S(1)}, f32[1,8,128]{2,1,0:T(8,128)}, u32[]{:S(2)}) copy-start(f32[1,8,128]{2,1,0:T(8,128)} %copy-done.10) | copy-start | bytes 12292
  129.3 4.9 %copy-start.13 = (f32[1,8,128]{2,1,0:T(8,128)S(1)}, f32[1,8,128]{2,1,0:T(8,128)}, u32[]{:S(2)}) copy-start(f32[1,8,128]{2,1,0:T(8,128)} %copy-done.12) | copy-start | bytes 12292
  130.5 4.3 %copy-start.14 = (f32[1,8,128]{2,1,0:T(8,128)}, f32[1,8,128]{2,1,0:T(8,128)S(1)}, u32[]{:S(2)}) copy-start(f32[1,8,128]{2,1,0:T(8,128)S(1)} %copy.411) | copy-start | bytes 12292
  131.8 3.1 %copy-start.15 = (f32[1,8,128]{2,1,0:T(8,128)}, f32[1,8,128]{2,1,0:T(8,128)S(1)}, u32[]{:S(2)}) copy-start(f32[1,8,128]{2,1,0:T(8,128)S(1)} %copy.414) | copy-start | bytes 12292
  131.8 2.5 %copy-start.7 = (f32[1,8,128]{2,1,0:T(8,128)S(1)}, f32[1,8,128]{2,1,0:T(8,128)}, u32[]{:S(2)}) copy-start(f32[1,8,128]{2,1,0:T(8,128)} %copy-done.6) | copy-start | bytes 12292
  131.8 2.5 %copy-start.9 = (f32[1,8,128]{2,1,0:T(8,128)S(1)}, f32[1,8,128]{2,1,0:T(8,128)}, u32[]{:S(2)}) copy-start(f32[1,8,128]{2,1,0:T(8,128)} %copy-done.8) | copy-start | bytes 12292
  133.0 1.9 copy-start.16
  133.2 1.7 copy-start.17
  133.5 1.1 copy-start.28
  133.5 1.1 copy-start.36
  133.9 1.8 copy-start.20
  133.9 1.8 copy-start.21
  134.2 1.6 copy-start.18
  134.2 1.6 copy-start.19
  134.4 5.1 %copy-start.4 = (f32[8,4,2,1,128]{4,0,2,1,3:T(8,128)S(1)}, f32[8,4,2,1,128]{4,0,2,1,3:T(8,128)}, u32[]{:S(2)}) copy-start(f32[8,4,2,1,128]{4,0,2,1,3:T(8,128)} %copy-done.3) | copy-start | bytes 98308
  139.4 0.8 copy-start.34
  141.2 62.5 %copy-start.31 = (pred[128]{0:T(512)(128)(4,1)S(1)}, pred[128]{0:T(512)(128)(4,1)}, u32[]{:S(2)}) copy-start(pred[128]{0:T(512)(128)(4,1)} %copy-done.30) | copy-start | bytes 388
  141.2 62.5 %copy-start.24 = (pred[128]{0:T(512)(128)(4,1)S(1)}, pred[128]{0:T(512)(128)(4,1)}, u32[]{:S(2)}) copy-start(pred[128]{0:T(512)(128)(4,1)} %copy-done.23) | copy-start | bytes 388
  141.2 58.1 %all-reduce.11.cloned.1.call-start = ((), (), s32[]{:S(2)}) async-start(), calls=%async_computation.4 | async-start | bytes 262144 | tf_op jit(solution)/shard_map/psum | solution.py:17
  209.1 4.5 %copy-start.5 = (f32[8,4,2,1,128]{4,0,2,1,3:T(8,128)S(1)}, f32[8,4,2,1,128]{4,0,2,1,3:T(8,128)}, u32[]{:S(2)}) copy-start(f32[8,4,2,1,128]{4,0,2,1,3:T(8,128)} %copy-done.3) | copy-start | bytes 98308
  209.1 4.5 %copy-start.29 = (f32[128]{0:T(128)S(1)}, f32[128]{0:T(128)}, u32[]{:S(2)}) copy-start(f32[128]{0:T(128)} %copy-done.27) | copy-start | bytes 1540
Sparse Core Ops, SparseCore 0:
  54.2 22.9 all-reduce.4
  81.9 31.9 all-reduce.6
  141.3 21.1 all-reduce.8
  167.3 31.9 all-reduce.10
